TPU v7x, 32 devices: a whole 2x2x4 slice. The times are simulated.
32 devices in a mesh: ctx: 16 (over z, x, core), head: 2 (over y).
Axes of the slice: x: 2, y: 2, z: 4, core: 2. Of those that a mesh axis runs over, the one named last changes fastest.
Arguments:
- queries: bfloat16 [4096, 8192], P(('ctx', 'head')), may hold values from -6 to 6
- key_heads: bfloat16 [4096, 1024], P(('ctx', 'head')), may hold values from -6 to 6
- value_head_array: bfloat16 [4096, 1024], P(('ctx', 'head')), may hold values from -6 to 6
- out_grad: bfloat16 [4096, 8192], P(('ctx', 'head')), may hold values from -6 to 6
- doc_ids: int32 [4096], P('ctx'), may hold values from 0 to 63, never falling along the last dimension, each value on 1 to 1792 neighbouring positions
Outputs:
- attended: bfloat16 [4096, 8192], P(('ctx', 'head'))
- query_grad: bfloat16 [4096, 8192], P(('ctx', 'head'))
- key_grad: bfloat16 [4096, 1024], P(('ctx', 'head'))
- value_grad: bfloat16 [4096, 1024], P(('ctx', 'head'))
Inputs may be any that keep to these rules, and one draw needn't show every extreme that they name: `doc_ids`: document numbers never fall along the batch; each document holds 1 to 1792 consecutive tokens and one holds exactly 1792.
All inputs are finite; a program needn't handle non-finite values.
Results may differ from a plain program's by a relative error of at most 0.022.
Values may be sent and summed in bfloat16 or wider, within the bound.
A program may use at most 192 MiB of HBM per device.

v0:
```python
import functools
import math

import jax
import jax.numpy as jnp
from jax import lax
from jax.experimental import pallas as pl
from jax.experimental.pallas import tpu as pltpu
from jax.sharding import PartitionSpec as P

HEAD_SIZE = 128
WINDOW = 1536
MASKED = -1e30
MESH = pl.DeviceIdType.MESH
VMEM = pl.BlockSpec(memory_space=pltpu.VMEM)


def remote(src, dst, send_sem, recv_sem, ctx, head):
    return pltpu.make_async_remote_copy(
        src_ref=src,
        dst_ref=dst,
        send_sem=send_sem,
        recv_sem=recv_sem,
        device_id={"ctx": ctx, "head": head},
        device_id_type=MESH,
    )


def greet(pairs, heads, back):
    ctx, head = lax.axis_index("ctx"), lax.axis_index("head")
    pair, core = ctx // 2, ctx % 2
    barrier = pltpu.get_barrier_semaphore()

    def signal(to_ctx, to_head):
        pl.semaphore_signal(
            barrier, inc=1, device_id={"ctx": to_ctx, "head": to_head}, device_id_type=MESH
        )

    signal(pair * 2 + 1 - core, head)
    for d in range(1, heads):
        signal(ctx, lax.rem(head + d, heads))
    for k in range(1, back + 1):
        for other in (pair + k, pair + pairs - k):
            signal(lax.rem(other, pairs) * 2 + core, head)
    pl.semaphore_wait(barrier, heads + 2 * back)


def gather_kernel(
    pairs, heads, back,
    q_ref, g_ref, kv_ref, doc_ref,
    q2, g2, win, docs,
    local_sem, core_send, core_recv, far_send, far_recv, head_send, head_recv, doc_send, doc_recv,
):
    ctx, head = lax.axis_index("ctx"), lax.axis_index("head")
    pair, core = ctx // 2, ctx % 2
    rows = q_ref.shape[0]
    half = q_ref.shape[1] // 2
    partner = pair * 2 + 1 - core
    mine = pl.ds(pl.multiple_of(head * rows, rows), rows)
    keep = pl.ds(pl.multiple_of(core * half, half), half)
    give = pl.ds(pl.multiple_of((1 - core) * half, half), half)

    def region(k, where=mine):
        return win.at[:, :, back - k, :, where, :]

    greet(pairs, heads, back)
    to_core = [
        remote(kv_ref.at[1 - core], win.at[:, :, back, core, mine, :], core_send.at[0], core_recv.at[0], partner, head),
        remote(doc_ref, docs.at[back, core], core_send.at[1], core_recv.at[1], partner, head),
        remote(q_ref.at[:, give], q2.at[core], core_send.at[2], core_recv.at[2], partner, head),
        remote(g_ref.at[:, give], g2.at[core], core_send.at[3], core_recv.at[3], partner, head),
    ]
    on_chip = [
        pltpu.make_async_copy(kv_ref.at[core], win.at[:, :, back, core, mine, :], local_sem.at[0]),
        pltpu.make_async_copy(doc_ref, docs.at[back, core], local_sem.at[1]),
        pltpu.make_async_copy(q_ref.at[:, keep], q2.at[core], local_sem.at[2]),
        pltpu.make_async_copy(g_ref.at[:, keep], g2.at[core], local_sem.at[3]),
    ]
    for copy in to_core + on_chip:
        copy.start()
    for k in range(1, back + 1):

        @pl.when(pair - k < 0)
        def _():
            win[:, :, back - k] = jnp.zeros(win.shape[:2] + win.shape[3:], win.dtype)
            docs[back - k] = jnp.full(docs.shape[1:], -1, docs.dtype)

    for n in range(2):
        on_chip[n].wait()
        to_core[n].wait_recv()

    def spread(k, d):
        return remote(
            region(k), region(k), head_send.at[d - 1, k], head_recv.at[d - 1, k],
            ctx, lax.rem(head + d, heads),
        )

    def ahead(k):
        to = ctx + 2 * k
        return (
            remote(region(0), region(k), far_send.at[k - 1], far_recv.at[k - 1], to, head),
            remote(docs.at[back], docs.at[back - k], doc_send.at[k - 1], doc_recv.at[k - 1], to, head),
        )

    for k in range(1, back + 1):

        @pl.when(pair + k < pairs)
        def _():
            for copy in ahead(k):
                copy.start()

    for d in range(1, heads):
        spread(0, d).start()
    for k in range(1, back + 1):

        @pl.when(pair - k >= 0)
        def _():
            for copy in ahead(k):
                copy.wait_recv()
            for d in range(1, heads):
                spread(k, d).start()

    for n in range(2, 4):
        on_chip[n].wait()
        to_core[n].wait_recv()
    for d in range(1, heads):
        spread(0, d).wait()
    for k in range(1, back + 1):

        @pl.when(pair - k >= 0)
        def _():
            for d in range(1, heads):
                spread(k, d).wait()

        @pl.when(pair + k < pairs)
        def _():
            for copy in ahead(k):
                copy.wait_send()

    for copy in to_core:
        copy.wait_send()


def attend_kernel(rows, heads_at_once, low_ref, q2, g2, win, out2, dq2, dkv, bias, acc):
    kv_heads, span = win.shape[1], win.shape[2]
    slots = q2.shape[0]
    group = q2.shape[2] // HEAD_SIZE // kv_heads
    block = (span - WINDOW) // slots
    length = WINDOW + rows
    scale = HEAD_SIZE ** (-0.5)
    factor = scale * math.log2(math.e)
    head = lax.axis_index("head")
    width = heads_at_once * HEAD_SIZE
    steps = group // heads_at_once

    def start_of(slot):
        return pl.multiple_of(slot * block + head * rows, rows)

    for slot in range(slots):
        key = start_of(slot) + lax.broadcasted_iota(jnp.int32, (length, rows), 0)
        own = start_of(slot) + WINDOW + lax.broadcasted_iota(jnp.int32, (length, rows), 1)
        bias[slot] = jnp.where((key >= low_ref[slot]) & (key <= own), 0.0, MASKED)

    def one_head(g, unused):
        acc[...] = jnp.zeros_like(acc)

        def one_step(step, unused):
            slot = step // steps
            first = pl.multiple_of(g * (group * HEAD_SIZE) + (step % steps) * width, width)
            keys_at = pl.ds(start_of(slot), length)
            keys, values = win[0, g, keys_at, :], win[1, g, keys_at, :]

            def stacked(ref):
                wide = ref[slot, :, pl.ds(first, width)]
                return jnp.concatenate(
                    [wide[:, n * HEAD_SIZE:(n + 1) * HEAD_SIZE] for n in range(heads_at_once)], axis=0
                )

            query, grad = stacked(q2), stacked(g2)
            nt = (((1,), (1,)), ((), ()))
            tn = (((0,), (0,)), ((), ()))
            f32 = jnp.float32
            scores = lax.dot_general(keys, query, nt, preferred_element_type=f32)
            shift = bias[slot]
            scores = scores * factor + jnp.concatenate([shift] * heads_at_once, axis=1)
            top = jnp.max(scores, axis=0, keepdims=True)
            probs = jnp.exp2(scores - top)
            total = jnp.sum(probs, axis=0, keepdims=True)
            probs = probs * (1.0 / total)
            weights = probs.astype(jnp.bfloat16)
            out = lax.dot_general(values, weights, tn, preferred_element_type=f32)
            out = out.astype(jnp.bfloat16).astype(f32)
            delta = jnp.sum(out * grad.astype(f32).T, axis=0, keepdims=True)
            prob_grad = lax.dot_general(values, grad, nt, preferred_element_type=f32)
            score_grad = (probs * (prob_grad - delta)).astype(jnp.bfloat16)
            dq = lax.dot_general(keys, score_grad, tn, preferred_element_type=f32) * scale
            acc[0, keys_at, :] += jnp.dot(score_grad, query, preferred_element_type=f32)
            acc[1, keys_at, :] += jnp.dot(weights, grad, preferred_element_type=f32)
            out_rows, dq_rows = out.T.astype(jnp.bfloat16), dq.T.astype(jnp.bfloat16)
            for n in range(heads_at_once):
                at = pl.ds(pl.multiple_of(first + n * HEAD_SIZE, HEAD_SIZE), HEAD_SIZE)
                out2[slot, :, at] = out_rows[n * rows:(n + 1) * rows]
                dq2[slot, :, at] = dq_rows[n * rows:(n + 1) * rows]
            return 0

        lax.fori_loop(0, slots * steps, one_step, 0)
        dkv[0, g] = (acc[0] * scale).astype(jnp.bfloat16)
        dkv[1, g] = acc[1].astype(jnp.bfloat16)
        return 0

    lax.fori_loop(0, kv_heads, one_head, 0)


def scatter_kernel(
    pairs, heads, back,
    out2, dq2, dkv,
    out, dq, result,
    passed, arrived, summed, far, total,
    local_sem, core_send, core_recv, far_send, far_recv, head_send, head_recv,
):
    ctx, head = lax.axis_index("ctx"), lax.axis_index("head")
    pair, core = ctx // 2, ctx % 2
    rows = out.shape[0]
    half = out.shape[1] // 2
    partner = pair * 2 + 1 - core
    keep = pl.ds(pl.multiple_of(core * half, half), half)
    f32 = jnp.float32

    def at(h):
        return pl.ds(pl.multiple_of(h * rows, rows), rows)

    greet(pairs, heads, back)

    def collect(k, d):
        to = lax.rem(head + d, heads)
        return remote(
            dkv.at[:, :, back - k, :, at(to), :], arrived.at[d - 1, k],
            head_send.at[d - 1, k], head_recv.at[d - 1, k], ctx, to,
        )

    def behind(k):
        return remote(summed.at[k], far.at[k - 1], far_send.at[k - 1], far_recv.at[k - 1], ctx - 2 * k, head)

    for k in range(back, -1, -1):

        @pl.when(pair - k >= 0)
        def _():
            for d in range(1, heads):
                collect(k, d).start()

    to_core = [
        remote(out2.at[1 - core], out.at[:, keep], core_send.at[0], core_recv.at[0], partner, head),
        remote(dq2.at[1 - core], dq.at[:, keep], core_send.at[1], core_recv.at[1], partner, head),
    ]
    on_chip = [
        pltpu.make_async_copy(out2.at[core], out.at[:, keep], local_sem.at[0]),
        pltpu.make_async_copy(dq2.at[core], dq.at[:, keep], local_sem.at[1]),
    ]
    for copy in to_core + on_chip:
        copy.start()
    for k in range(back, -1, -1):

        @pl.when(pair - k >= 0)
        def _():
            part = dkv[:, :, back - k, :, at(head), :].astype(f32)
            for d in range(1, heads):
                collect(k, d).wait_recv()
                part = part + arrived[d - 1, k].astype(f32)
            summed[k] = part.astype(jnp.bfloat16)
            if k > 0:
                behind(k).start()

    passed[...] = summed[0].astype(f32)
    for k in range(1, back + 1):

        @pl.when(pair + k < pairs)
        def _():
            behind(k).wait_recv()
            passed[...] = passed[...] + far[k - 1].astype(f32)

    total[...] = passed[...].astype(jnp.bfloat16)
    last = [
        remote(total.at[:, :, 1 - core], result.at[core], core_send.at[2], core_recv.at[2], partner, head),
        pltpu.make_async_copy(total.at[:, :, core], result.at[core], local_sem.at[2]),
    ]
    for copy in last:
        copy.start()
    for k in range(back, -1, -1):

        @pl.when(pair - k >= 0)
        def _():
            for d in range(1, heads):
                collect(k, d).wait_send()
            if k > 0:
                behind(k).wait_send()

    for copy in to_core + on_chip + last:
        copy.wait()


def local(pairs, heads, queries, key_heads, value_head_array, out_grad, doc_ids):
    rows, width = queries.shape
    kv_heads = key_heads.shape[1] // HEAD_SIZE
    half_kv = kv_heads // 2
    block = doc_ids.shape[0]
    back = -(-WINDOW // (2 * block))
    bf16, f32 = jnp.bfloat16, jnp.float32
    DMA = pltpu.SemaphoreType.DMA
    params = functools.partial(pltpu.CompilerParams, vmem_limit_bytes=60 * 1024 * 1024)

    kv = jnp.stack([key_heads, value_head_array]).reshape(2, rows, 2, half_kv, HEAD_SIZE)
    kv = jnp.transpose(kv, (2, 0, 3, 1, 4))
    docs_here = doc_ids.reshape(1, block)
    two = jax.ShapeDtypeStruct((2, rows, width // 2), bf16)
    window = jax.ShapeDtypeStruct((2, half_kv, back + 1, 2, block, HEAD_SIZE), bf16)
    q2, g2, win, docs = pl.pallas_call(
        functools.partial(gather_kernel, pairs, heads, back),
        out_shape=(two, two, window, jax.ShapeDtypeStruct((back + 1, 2, 1, block), jnp.int32)),
        in_specs=[VMEM] * 4,
        out_specs=(VMEM,) * 4,
        scratch_shapes=[
            DMA((4,)), DMA((4,)), DMA((4,)), DMA((back,)), DMA((back,)),
            DMA((heads - 1, back + 1)), DMA((heads - 1, back + 1)), DMA((back,)), DMA((back,)),
        ],
        compiler_params=params(collective_id=0, has_side_effects=True),
    )(queries, out_grad, kv, docs_here)

    span = (back + 1) * 2 * block
    doc_keys = docs.reshape(span)
    head = lax.axis_index("head")
    doc_rows = lax.dynamic_slice_in_dim(docs[back, :, 0, :], head * rows, rows, 1)
    at = jnp.arange(span, dtype=jnp.int32)
    own = WINDOW + (jnp.arange(2, dtype=jnp.int32) * block)[:, None] + head * rows + jnp.arange(rows, dtype=jnp.int32)
    earlier = (doc_rows[:, :, None] == doc_keys) & (at < own[:, :, None])
    first = own - jnp.sum(earlier.astype(jnp.int32), axis=-1)
    low = jnp.maximum(first, own - (WINDOW - 1)).reshape(2, 1, rows)

    length = WINDOW + rows
    out2, dq2, dkv = pl.pallas_call(
        functools.partial(attend_kernel, rows, 2),
        out_shape=(two, two, jax.ShapeDtypeStruct((2, half_kv, span, HEAD_SIZE), bf16)),
        in_specs=[VMEM] * 4,
        out_specs=(VMEM,) * 3,
        scratch_shapes=[pltpu.VMEM((2, length, rows), f32), pltpu.VMEM((2, span, HEAD_SIZE), f32)],
        compiler_params=params(),
    )(low, q2, g2, win.reshape(2, half_kv, span, HEAD_SIZE))

    piece = (2, half_kv, 2, rows, HEAD_SIZE)
    whole = jax.ShapeDtypeStruct((rows, width), bf16)
    out, dq, result = pl.pallas_call(
        functools.partial(scatter_kernel, pairs, heads, back),
        out_shape=(whole, whole, jax.ShapeDtypeStruct((2, 2, half_kv, rows, HEAD_SIZE), bf16)),
        in_specs=[VMEM] * 3,
        out_specs=(VMEM,) * 3,
        scratch_shapes=[
            pltpu.VMEM(piece, f32),
            pltpu.VMEM((heads - 1, back + 1) + piece, bf16),
            pltpu.VMEM((back + 1,) + piece, bf16),
            pltpu.VMEM((back,) + piece, bf16),
            pltpu.VMEM(piece, bf16),
            DMA((3,)), DMA((3,)), DMA((3,)), DMA((back,)), DMA((back,)),
            DMA((heads - 1, back + 1)), DMA((heads - 1, back + 1)),
        ],
        compiler_params=params(collective_id=1, has_side_effects=True),
    )(out2, dq2, dkv.reshape(window.shape))
    both = jnp.transpose(result, (1, 3, 0, 2, 4)).reshape(2, rows, kv_heads * HEAD_SIZE)
    return (out, dq, both[0], both[1])


def solution(mesh):
    tokens = P(("ctx", "head"), None)
    return jax.shard_map(
        functools.partial(local, mesh.shape["ctx"] // 2, mesh.shape["head"]),
        mesh=mesh,
        in_specs=(tokens, tokens, tokens, tokens, P("ctx")),
        out_specs=(tokens, tokens, tokens, tokens),
        check_vma=False,
    )
```

profile of v0, /device:TPU:15, one launch (start us, length us, event | category | flops | bytes accessed | tf_op | source)
XLA Modules:
  0.0 238.3 jit_solution(2944167765723740216)
XLA Ops:
  0.6 0.1 iota_add_fusion
  0.7 1.1 copy.17
  1.8 0.2 copy.19
  2.0 1.1 copy.18
  3.2 0.2 copy.20
  3.3 0.8 maximum_bitcast_fusion.kv_ref
  4.2 59.1 %shard_map.84 = (bf16[2,128,4096]{2,1,0:T(8,128)(2,1)}, bf16[2,128,4096]{2,1,0:T(8,128)(2,1)}, bf16[2,4,4,2,256,128]{5,4,3,2,1,0:T(8,128)(2,1)}, s32[4,2,1,256]{3,2,1,0:T(1,128)}) custom-call(bf16[128,8192]{1,0:T(8,128)(2,1)} %q_ref.1, bf16[128,8192]{1,0:T(8,128)(2,1)} %g_ref.1, bf16[2,2,4,128,128]{4,3,2,1,0:T(8,128)(2,1)} %maximum_bitcast_fusion.kv_ref, ...), custom_call_target="tpu_custom_call" | custom-call | tf_op jit(solution)/shard_map/pallas_call | solution.py:316
  63.2 0.7 slice.11
  63.9 1.2 convert_reduce_fusion
  65.2 0.6 add_maximum_fusion.low_ref
  65.8 86.7 %shard_map.85 = (bf16[2,128,4096]{2,1,0:T(8,128)(2,1)}, bf16[2,128,4096]{2,1,0:T(8,128)(2,1)}, bf16[2,4,2048,128]{3,2,1,0:T(8,128)(2,1)}) custom-call(s32[2,1,128]{2,1,0:T(1,128)} %add_maximum_fusion.low_ref, bf16[2,128,4096]{2,1,0:T(8,128)(2,1)} %get-tuple-element.15.q2, bf16[2,128,4096]{2,1,0:T(8,128)(2,1)} %get-tuple-element.16.g2, ...), custom_call_target="tpu_custom_call" | custom-call | tf_op jit(solution)/shard_map/pallas_call | solution.py:339
  152.5 78.8 %shard_map.86 = (bf16[128,8192]{1,0:T(8,128)(2,1)}, bf16[128,8192]{1,0:T(8,128)(2,1)}, bf16[2,2,4,128,128]{4,3,2,1,0:T(8,128)(2,1)}) custom-call(bf16[2,128,4096]{2,1,0:T(8,128)(2,1)} %get-tuple-element.18.out2, bf16[2,128,4096]{2,1,0:T(8,128)(2,1)} %get-tuple-element.19.dq2, bf16[2,4,4,2,256,128]{5,4,3,2,1,0:T(8,128)(2,1)} %bitcast.14), custom_call_target="tpu_custom_call" | custom-call | tf_op jit(solution)/shard_map/pallas_call | solution.py:350
  231.4 0.0 copy-start.1
  231.4 1.2 fusion.1
  232.6 0.2 copy.22
  232.8 0.9 copy.24
  233.6 0.2 copy.21
  233.8 0.9 copy.23
  234.7 0.0 copy-done.1
  234.7 0.0 copy-start
  234.7 1.3 copy.27
  236.0 1.0 copy-done
  237.0 1.3 copy.28
  (2 shorter events, 0.0 us)
Async XLA Ops:
  231.4 3.3 %copy-start.1 = (bf16[128,8192]{1,0:T(8,128)(2,1)S(1)}, bf16[128,8192]{1,0:T(8,128)(2,1)}, u32[]{:S(2)}) copy-start(bf16[128,8192]{1,0:T(8,128)(2,1)} %get-tuple-element.38) | copy-start | bytes 6291460
  234.7 2.3 copy-start
where the time goes:
time: 239 us; the launch traced here: 238 us
  Pallas kernels  225 us (94%)
  local copies, waits for them, and re-layouts  10.2 us (4%)
  other arithmetic  2.81 us (1%)
    pallas_call x1, Pallas kernels, local(): pl.pallas_call(functools.partial(attend_kernel, rows, 2), out_shape=(two,...  86.7 us
    pallas_call x1, Pallas kernels, local(): pl.pallas_call(functools.partial(scatter_kernel, pairs, heads, back), out...  78.8 us
    pallas_call x1, Pallas kernels, local(): pl.pallas_call(functools.partial(gather_kernel, pairs, heads, back), out_...  59.1 us
    unnamed x10, local copies, waits for them, and re-layouts  7.62 us

commit v1 on v0

v1 whole, which is shorter than its diff:
```python
import functools
import math

import jax
import jax.numpy as jnp
from jax import lax
from jax.experimental import pallas as pl
from jax.experimental.pallas import tpu as pltpu
from jax.sharding import PartitionSpec as P

HEAD_SIZE = 128
WINDOW = 1536
MASKED = -1e30
MESH = pl.DeviceIdType.MESH
VMEM = pl.BlockSpec(memory_space=pltpu.VMEM)


def remote(src, dst, send_sem, recv_sem, ctx, head):
    return pltpu.make_async_remote_copy(
        src_ref=src,
        dst_ref=dst,
        send_sem=send_sem,
        recv_sem=recv_sem,
        device_id={"ctx": ctx, "head": head},
        device_id_type=MESH,
    )


def greet(pairs, heads, back):
    ctx, head = lax.axis_index("ctx"), lax.axis_index("head")
    pair, core = ctx // 2, ctx % 2
    barrier = pltpu.get_barrier_semaphore()

    def signal(to_ctx, to_head):
        pl.semaphore_signal(
            barrier, inc=1, device_id={"ctx": to_ctx, "head": to_head}, device_id_type=MESH
        )

    signal(pair * 2 + 1 - core, head)
    for d in range(1, heads):
        signal(ctx, lax.rem(head + d, heads))
    for k in range(1, back + 1):
        for other in (pair + k, pair + pairs - k):
            signal(lax.rem(other, pairs) * 2 + core, head)
    pl.semaphore_wait(barrier, heads + 2 * back)


def fused_kernel(
    pairs, heads, back, heads_at_once,
    q_ref, g_ref, kv_ref, doc_ref,
    out, dq, result,
    q2, g2, win, docs, key_docs, bias, acc, out2, dq2, dkv, arrived, summed, far, total,
    local_sem, core_send, core_recv, doc_send, doc_recv,
    far_send, far_recv, head_send, head_recv,
    part_send, part_recv, back_send, back_recv, out_send, out_recv, out_local,
):
    ctx, head = lax.axis_index("ctx"), lax.axis_index("head")
    pair, core = ctx // 2, ctx % 2
    rows = q_ref.shape[0]
    half = q_ref.shape[1] // 2
    slots, block = 2, docs.shape[-1]
    kv_heads = win.shape[1]
    span = (back + 1) * slots * block
    group = half // HEAD_SIZE // kv_heads
    partner = pair * 2 + 1 - core
    length = WINDOW + rows
    scale = HEAD_SIZE ** (-0.5)
    factor = scale * math.log2(math.e)
    width = heads_at_once * HEAD_SIZE
    steps = group // heads_at_once
    f32, bf16 = jnp.float32, jnp.bfloat16
    flat = win.reshape(2, kv_heads, span, HEAD_SIZE)

    def at(h):
        return pl.ds(pl.multiple_of(h * rows, rows), rows)

    def columns(which, g=None):
        if g is None:
            return pl.ds(pl.multiple_of(which * half, half), half)
        size = group * HEAD_SIZE
        return pl.ds(pl.multiple_of(which * half + g * size, size), size)

    mine = at(head)

    def region(k, g):
        return win.at[:, g, back - k, :, mine, :]

    def ahead(k, g):
        return remote(region(0, g), region(k, g), far_send.at[k - 1, g], far_recv.at[k - 1, g], ctx + 2 * k, head)

    def ahead_docs(k):
        return remote(docs.at[back], docs.at[back - k], doc_send.at[k - 1], doc_recv.at[k - 1], ctx + 2 * k, head)

    def spread(k, d, g):
        return remote(
            region(k, g), region(k, g), head_send.at[d - 1, k, g], head_recv.at[d - 1, k, g],
            ctx, lax.rem(head + d, heads),
        )

    def collect(k, d, g):
        to = lax.rem(head + d, heads)
        return remote(
            dkv.at[:, g, back - k, :, at(to), :], arrived.at[d - 1, k, g],
            part_send.at[d - 1, k, g], part_recv.at[d - 1, k, g], ctx, to,
        )

    def behind(k, g):
        return remote(summed.at[k, g], far.at[k - 1, g], back_send.at[k - 1, g], back_recv.at[k - 1, g], ctx - 2 * k, head)

    def returned(g):
        copies = []
        for n, (src, dst) in enumerate(((out2, out), (dq2, dq))):
            to = dst.at[:, columns(core, g)]
            copies.append(remote(src.at[1 - core, :, columns(0, g)], to, out_send.at[n, g], out_recv.at[n, g], partner, head))
            copies.append(pltpu.make_async_copy(src.at[core, :, columns(0, g)], to, out_local.at[n, g]))
        return copies

    def each(make, lower, upper):
        for k in range(1, back + 1):
            if lower:
                pl.when(pair - k >= 0)(functools.partial(make, k))
            if upper:
                pl.when(pair + k < pairs)(functools.partial(make, k))

    greet(pairs, heads, back)
    to_core = [
        remote(doc_ref, docs.at[back, core], core_send.at[0], core_recv.at[0], partner, head),
        remote(kv_ref.at[1 - core], win.at[:, :, back, core, mine, :], core_send.at[1], core_recv.at[1], partner, head),
        remote(q_ref.at[:, columns(1 - core)], q2.at[core], core_send.at[2], core_recv.at[2], partner, head),
        remote(g_ref.at[:, columns(1 - core)], g2.at[core], core_send.at[3], core_recv.at[3], partner, head),
    ]
    on_chip = [
        pltpu.make_async_copy(doc_ref, docs.at[back, core], local_sem.at[0]),
        pltpu.make_async_copy(kv_ref.at[core], win.at[:, :, back, core, mine, :], local_sem.at[1]),
        pltpu.make_async_copy(q_ref.at[:, columns(core)], q2.at[core], local_sem.at[2]),
        pltpu.make_async_copy(g_ref.at[:, columns(core)], g2.at[core], local_sem.at[3]),
    ]
    for copy in to_core + on_chip:
        copy.start()
    for k in range(1, back + 1):

        @pl.when(pair - k < 0)
        def _():
            win[:, :, back - k] = jnp.zeros(win.shape[:2] + win.shape[3:], win.dtype)
            docs[back - k] = jnp.full(docs.shape[1:], -1, docs.dtype)

    for n in range(2):
        on_chip[n].wait()
        to_core[n].wait_recv()
    each(lambda k: ahead_docs(k).start(), False, True)

    def send_keys(g, unused):
        each(lambda k: ahead(k, g).start(), False, True)
        for d in range(1, heads):
            spread(0, d, g).start()
        return 0

    lax.fori_loop(0, kv_heads, send_keys, 0)

    def forward(g):
        def one(k):
            ahead(k, g).wait_recv()
            for d in range(1, heads):
                spread(k, d, g).start()

        each(one, True, False)

    def ready(g):
        for d in range(1, heads):
            spread(0, d, g).wait()

        def one(k):
            for d in range(1, heads):
                spread(k, d, g).wait()

        each(one, True, False)

    def reduce_parts(g):
        for k in range(back, -1, -1):

            @pl.when(pair - k >= 0)
            def _():
                part = dkv[:, g, back - k, :, mine, :].astype(f32)
                for d in range(1, heads):
                    collect(k, d, g).wait_recv()
                    part = part + arrived[d - 1, k, g].astype(f32)
                summed[k, g] = part.astype(bf16)
                if k > 0:
                    behind(k, g).start()

    def finish(g):
        acc_here = acc.at[:, pl.ds(0, slots * rows), :]
        acc_here[...] = summed[0, g].astype(f32).reshape(acc_here.shape)

        def one(k):
            behind(k, g).wait_recv()
            acc_here[...] = acc_here[...] + far[k - 1, g].astype(f32).reshape(acc_here.shape)

        each(one, False, True)
        total[:, g] = acc_here[...].astype(bf16).reshape(2, slots, rows, HEAD_SIZE)

    each(lambda k: ahead_docs(k).wait_recv(), True, False)
    tile = 128
    for k in range(back + 1):
        for slot in range(slots):
            for n in range(block // tile):
                row = docs[k, slot, :, n * tile:(n + 1) * tile].astype(f32)
                column = jnp.broadcast_to(row, (tile, tile)).T
                key_docs[pl.ds((k * slots + slot) * block + n * tile, tile), :] = column[:, :rows]

    def start_of(slot):
        return pl.multiple_of(slot * block + head * rows, rows)

    for slot in range(slots):
        query_doc = docs[back, slot, :, 0:rows]
        for h in range(1, heads):
            query_doc = jnp.where(head == h, docs[back, slot, :, h * rows:(h + 1) * rows], query_doc)
        apart = lax.broadcasted_iota(jnp.int32, (length, rows), 1) + WINDOW - lax.broadcasted_iota(jnp.int32, (length, rows), 0)
        same = key_docs[pl.ds(start_of(slot), length), :] == query_doc.astype(f32)
        bias[slot] = jnp.where(same & (apart >= 0) & (apart < WINDOW), 0.0, MASKED)

    forward(0)
    for n in range(2, 4):
        on_chip[n].wait()
        to_core[n].wait_recv()

    def one_head(g, unused):
        ready(g)

        @pl.when(g + 1 < kv_heads)
        def _():
            forward(g + 1)

        @pl.when(g >= 2)
        def _():
            finish(g - 2)

        acc[...] = jnp.zeros_like(acc)

        def one_slot(slot, unused):
            keys_at = pl.ds(start_of(slot), length)

            def one_step(step, unused):
                first = pl.multiple_of(g * (group * HEAD_SIZE) + step * width, width)
                keys, values = flat[0, g, keys_at, :], flat[1, g, keys_at, :]

                def stacked(ref):
                    wide = ref[slot, :, pl.ds(first, width)]
                    return jnp.concatenate(
                        [wide[:, n * HEAD_SIZE:(n + 1) * HEAD_SIZE] for n in range(heads_at_once)], axis=0
                    )

                query, grad = stacked(q2), stacked(g2)
                nt = (((1,), (1,)), ((), ()))
                tn = (((0,), (0,)), ((), ()))
                scores = lax.dot_general(keys, query, nt, preferred_element_type=f32)
                scores = scores * factor + jnp.concatenate([bias[slot]] * heads_at_once, axis=1)
                top = jnp.max(scores, axis=0, keepdims=True)
                probs = jnp.exp2(scores - top)
                probs = probs * (1.0 / jnp.sum(probs, axis=0, keepdims=True))
                weights = probs.astype(bf16)
                attended = lax.dot_general(values, weights, tn, preferred_element_type=f32)
                attended = attended.astype(bf16).astype(f32)
                delta = jnp.sum(attended * grad.astype(f32).T, axis=0, keepdims=True)
                prob_grad = lax.dot_general(values, grad, nt, preferred_element_type=f32)
                score_grad = (probs * (prob_grad - delta)).astype(bf16)
                query_grad = lax.dot_general(keys, score_grad, tn, preferred_element_type=f32) * scale
                acc[0, keys_at, :] += jnp.dot(score_grad, query, preferred_element_type=f32)
                acc[1, keys_at, :] += jnp.dot(weights, grad, preferred_element_type=f32)
                out_rows, dq_rows = attended.T.astype(bf16), query_grad.T.astype(bf16)
                for n in range(heads_at_once):
                    to = pl.ds(pl.multiple_of(first + n * HEAD_SIZE, HEAD_SIZE), HEAD_SIZE)
                    out2[slot, :, to] = out_rows[n * rows:(n + 1) * rows]
                    dq2[slot, :, to] = dq_rows[n * rows:(n + 1) * rows]
                return 0

            lax.fori_loop(0, steps, one_step, 0)

            @pl.when((slot == 0) & (g >= 1))
            def _():
                reduce_parts(g - 1)

            return 0

        lax.fori_loop(0, slots, one_slot, 0)
        dkv[0, g] = (acc[0] * scale).astype(bf16).reshape(dkv.shape[2:])
        dkv[1, g] = acc[1].astype(bf16).reshape(dkv.shape[2:])
        for k in range(back, -1, -1):

            @pl.when(pair - k >= 0)
            def _():
                for d in range(1, heads):
                    collect(k, d, g).start()

        for copy in returned(g):
            copy.start()
        return 0

    lax.fori_loop(0, kv_heads, one_head, 0)
    for g in range(max(kv_heads - 2, 0), kv_heads):
        if g == kv_heads - 1:
            reduce_parts(g)
        finish(g)
    last = [
        remote(total.at[:, :, 1 - core], result.at[core], core_send.at[4], core_recv.at[4], partner, head),
        pltpu.make_async_copy(total.at[:, :, core], result.at[core], local_sem.at[4]),
    ]
    for copy in last:
        copy.start()

    def drain(g, unused):
        for copy in returned(g):
            copy.wait()
        each(lambda k: ahead(k, g).wait_send(), False, True)
        for k in range(back + 1):

            @pl.when(pair - k >= 0)
            def _():
                for d in range(1, heads):
                    collect(k, d, g).wait_send()
                if k > 0:
                    behind(k, g).wait_send()

        return 0

    lax.fori_loop(0, kv_heads, drain, 0)
    each(lambda k: ahead_docs(k).wait_send(), False, True)
    for copy in to_core:
        copy.wait_send()
    for copy in last:
        copy.wait()


def local(pairs, heads, queries, key_heads, value_head_array, out_grad, doc_ids):
    rows, width = queries.shape
    kv_heads = key_heads.shape[1] // HEAD_SIZE
    half_kv = kv_heads // 2
    block = doc_ids.shape[0]
    back = -(-WINDOW // (2 * block))
    span = (back + 1) * 2 * block
    length = WINDOW + rows
    bf16, f32 = jnp.bfloat16, jnp.float32
    DMA = pltpu.SemaphoreType.DMA

    kv = jnp.stack([key_heads, value_head_array]).reshape(2, rows, 2, half_kv, HEAD_SIZE)
    kv = jnp.transpose(kv, (2, 0, 3, 1, 4))
    whole = jax.ShapeDtypeStruct((rows, width), bf16)
    two = pltpu.VMEM((2, rows, width // 2), bf16)
    window = pltpu.VMEM((2, half_kv, back + 1, 2, block, HEAD_SIZE), bf16)
    piece = (half_kv, 2, 2, rows, HEAD_SIZE)
    out, dq, result = pl.pallas_call(
        functools.partial(fused_kernel, pairs, heads, back, 2),
        out_shape=(whole, whole, jax.ShapeDtypeStruct((2, 2, half_kv, rows, HEAD_SIZE), bf16)),
        in_specs=[VMEM] * 4,
        out_specs=(VMEM,) * 3,
        scratch_shapes=[
            two, two, window,
            pltpu.VMEM((back + 1, 2, 1, block), jnp.int32),
            pltpu.VMEM((span, rows), f32),
            pltpu.VMEM((2, length, rows), f32),
            pltpu.VMEM((2, span, HEAD_SIZE), f32),
            two, two, window,
            pltpu.VMEM((heads - 1, back + 1) + piece, bf16),
            pltpu.VMEM((back + 1,) + piece, bf16),
            pltpu.VMEM((back,) + piece, bf16),
            pltpu.VMEM((2, half_kv, 2, rows, HEAD_SIZE), bf16),
            DMA((5,)), DMA((5,)), DMA((5,)), DMA((back,)), DMA((back,)),
            DMA((back, half_kv)), DMA((back, half_kv)),
            DMA((heads - 1, back + 1, half_kv)), DMA((heads - 1, back + 1, half_kv)),
            DMA((heads - 1, back + 1, half_kv)), DMA((heads - 1, back + 1, half_kv)),
            DMA((back, half_kv)), DMA((back, half_kv)),
            DMA((2, half_kv)), DMA((2, half_kv)), DMA((2, half_kv)),
        ],
        compiler_params=pltpu.CompilerParams(
            collective_id=0, has_side_effects=True, vmem_limit_bytes=63 * 1024 * 1024
        ),
    )(queries, out_grad, kv, doc_ids.reshape(1, block))
    both = jnp.transpose(result, (1, 3, 0, 2, 4)).reshape(2, rows, kv_heads * HEAD_SIZE)
    return (out, dq, both[0], both[1])


def solution(mesh):
    tokens = P(("ctx", "head"), None)
    return jax.shard_map(
        functools.partial(local, mesh.shape["ctx"] // 2, mesh.shape["head"]),
        mesh=mesh,
        in_specs=(tokens, tokens, tokens, tokens, P("ctx")),
        out_specs=(tokens, tokens, tokens, tokens),
        check_vma=False,
    )
```

time: 239 us -> 151 us (0.63)
  Pallas kernels: 225 us -> 137 us
    pallas_call x3 -> x1, Pallas kernels: 225 us -> 137 us  [local(): pl.pallas_call(functools.partial(fused_kernel, pairs, heads, back, 2), ou...]
where the time goes in v1:
time: 151 us; the launch traced here: 148 us
  Pallas kernels  137 us (91%)
  local copies, waits for them, and re-layouts  9.55 us (6%)
    pallas_call x1, Pallas kernels, local(): pl.pallas_call(functools.partial(fused_kernel, pairs, heads, back, 2), ou...  137 us
    unnamed x10, local copies, waits for them, and re-layouts  7.62 us

profile of v1, /device:TPU:15, one launch (start us, length us, event | category | flops | bytes accessed | tf_op | source)
XLA Modules:
  0.0 148.2 jit_solution(3574353866143359824)
XLA Ops:
  0.6 1.1 copy.9
  1.8 0.2 copy.11
  1.9 1.1 copy.10
  3.1 0.2 copy.12
  3.3 0.8 maximum_bitcast_fusion.kv_ref
  4.1 137.1 %shard_map.84 = (bf16[128,8192]{1,0:T(8,128)(2,1)}, bf16[128,8192]{1,0:T(8,128)(2,1)}, bf16[2,2,4,128,128]{4,3,2,1,0:T(8,128)(2,1)}) custom-call(bf16[128,8192]{1,0:T(8,128)(2,1)} %q_ref.1, bf16[128,8192]{1,0:T(8,128)(2,1)} %g_ref.1, bf16[2,2,4,128,128]{4,3,2,1,0:T(8,128)(2,1)} %maximum_bitcast_fusion.kv_ref, s32[1,256]{1,0:T(1,128)} %bitcast.13), custom_call_target="tpu_custom_call" | custom-call | tf_op jit(solution)/shard_map/pallas_call | solution.py:351
  141.2 0.0 copy-start.1
  141.2 1.2 fusion
  142.4 0.2 copy.14
  142.6 0.9 copy.16
  143.4 0.2 copy.13
  143.6 0.9 copy.15
  144.5 0.0 copy-done.1
  144.5 0.0 copy-start
  144.5 1.3 copy.19
  145.8 1.0 copy-done
  146.8 1.3 copy.20
Async XLA Ops:
  141.2 3.3 %copy-start.1 = (bf16[128,8192]{1,0:T(8,128)(2,1)S(1)}, bf16[128,8192]{1,0:T(8,128)(2,1)}, u32[]{:S(2)}) copy-start(bf16[128,8192]{1,0:T(8,128)(2,1)} %get-tuple-element.20) | copy-start | bytes 6291460
  144.5 2.3 %copy-start = (bf16[128,8192]{1,0:T(8,128)(2,1)S(1)}, bf16[128,8192]{1,0:T(8,128)(2,1)}, u32[]{:S(2)}) copy-start(bf16[128,8192]{1,0:T(8,128)(2,1)} %get-tuple-element.21) | copy-start | bytes 6291460

commit v2 on v1

--- a/solution.py
+++ b/solution.py
@@ -257,16 +257,17 @@
                 scores = scores * factor + jnp.concatenate([bias[slot]] * heads_at_once, axis=1)
                 top = jnp.max(scores, axis=0, keepdims=True)
                 probs = jnp.exp2(scores - top)
-                probs = probs * (1.0 / jnp.sum(probs, axis=0, keepdims=True))
+                inverse = 1.0 / jnp.sum(probs, axis=0, keepdims=True)
+                by_row = jnp.broadcast_to(inverse, (HEAD_SIZE, inverse.shape[1])).T
                 weights = probs.astype(bf16)
                 attended = lax.dot_general(values, weights, tn, preferred_element_type=f32)
-                attended = attended.astype(bf16).astype(f32)
+                attended = (attended * inverse).astype(bf16).astype(f32)
                 delta = jnp.sum(attended * grad.astype(f32).T, axis=0, keepdims=True)
                 prob_grad = lax.dot_general(values, grad, nt, preferred_element_type=f32)
                 score_grad = (probs * (prob_grad - delta)).astype(bf16)
-                query_grad = lax.dot_general(keys, score_grad, tn, preferred_element_type=f32) * scale
-                acc[0, keys_at, :] += jnp.dot(score_grad, query, preferred_element_type=f32)
-                acc[1, keys_at, :] += jnp.dot(weights, grad, preferred_element_type=f32)
+                query_grad = lax.dot_general(keys, score_grad, tn, preferred_element_type=f32) * (scale * inverse)
+                acc[0, keys_at, :] += jnp.dot(score_grad, (query.astype(f32) * by_row).astype(bf16), preferred_element_type=f32)
+                acc[1, keys_at, :] += jnp.dot(weights, (grad.astype(f32) * by_row).astype(bf16), preferred_element_type=f32)
                 out_rows, dq_rows = attended.T.astype(bf16), query_grad.T.astype(bf16)
                 for n in range(heads_at_once):
                     to = pl.ds(pl.multiple_of(first + n * HEAD_SIZE, HEAD_SIZE), HEAD_SIZE)
@@ -349,7 +350,7 @@
     window = pltpu.VMEM((2, half_kv, back + 1, 2, block, HEAD_SIZE), bf16)
     piece = (half_kv, 2, 2, rows, HEAD_SIZE)
     out, dq, result = pl.pallas_call(
-        functools.partial(fused_kernel, pairs, heads, back, 2),
+        functools.partial(fused_kernel, pairs, heads, back, 8),
         out_shape=(whole, whole, jax.ShapeDtypeStruct((2, 2, half_kv, rows, HEAD_SIZE), bf16)),
         in_specs=[VMEM] * 4,
         out_specs=(VMEM,) * 3,

time: 151 us -> 135 us (0.89)
  Pallas kernels: 137 us -> 122 us
    pallas_call x1, Pallas kernels: 137 us -> 122 us  [local(): pl.pallas_call(functools.partial(fused_kernel, pairs, heads, back, 8), ou...]
where the time goes in v2:
time: 135 us; the launch traced here: 133 us
  Pallas kernels  122 us (90%)
  local copies, waits for them, and re-layouts  9.55 us (7%)
    pallas_call x1, Pallas kernels, local(): pl.pallas_call(functools.partial(fused_kernel, pairs, heads, back, 8), ou...  122 us
    unnamed x10, local copies, waits for them, and re-layouts  7.62 us

profile of v2, /device:TPU:15, one launch (start us, length us, event | category | flops | bytes accessed | tf_op | source)
XLA Modules:
  0.0 132.9 jit_solution(16744343830576073365)
XLA Ops:
  0.6 1.1 copy.9
  1.8 0.2 copy.11
  1.9 1.1 copy.10
  3.1 0.2 copy.12
  3.3 0.8 maximum_bitcast_fusion.kv_ref
  4.1 121.9 %shard_map.84 = (bf16[128,8192]{1,0:T(8,128)(2,1)}, bf16[128,8192]{1,0:T(8,128)(2,1)}, bf16[2,2,4,128,128]{4,3,2,1,0:T(8,128)(2,1)}) custom-call(bf16[128,8192]{1,0:T(8,128)(2,1)} %q_ref.1, bf16[128,8192]{1,0:T(8,128)(2,1)} %g_ref.1, bf16[2,2,4,128,128]{4,3,2,1,0:T(8,128)(2,1)} %maximum_bitcast_fusion.kv_ref, s32[1,256]{1,0:T(1,128)} %bitcast.13), custom_call_target="tpu_custom_call" | custom-call | tf_op jit(solution)/shard_map/pallas_call | solution.py:352
  126.0 0.0 copy-start.1
  126.0 1.2 fusion
  127.2 0.2 copy.14
  127.4 0.9 copy.16
  128.2 0.2 copy.13
  128.4 0.9 copy.15
  129.3 0.0 copy-done.1
  129.3 0.0 copy-start
  129.3 1.3 copy.19
  130.6 1.0 copy-done
  131.6 1.3 copy.20
Async XLA Ops:
  126.0 3.3 %copy-start.1 = (bf16[128,8192]{1,0:T(8,128)(2,1)S(1)}, bf16[128,8192]{1,0:T(8,128)(2,1)}, u32[]{:S(2)}) copy-start(bf16[128,8192]{1,0:T(8,128)(2,1)} %get-tuple-element.20) | copy-start | bytes 6291460
  129.3 2.3 %copy-start = (bf16[128,8192]{1,0:T(8,128)(2,1)S(1)}, bf16[128,8192]{1,0:T(8,128)(2,1)}, u32[]{:S(2)}) copy-start(bf16[128,8192]{1,0:T(8,128)(2,1)} %get-tuple-element.21) | copy-start | bytes 6291460
